TPU v7x, 32 devices: a whole 2x2x4 slice. The times are simulated.
32 devices in a mesh: groups: 2 (over y), ctx: 4 (over z), tensor: 2 (over x), dp: 2 (over core).
Axes of the slice: x: 2, y: 2, z: 4, core: 2. Of those that a mesh axis runs over, the one named last changes fastest.
Arguments:
- tokens: bfloat16 [4, 1024, 1024], P(('groups', 'dp'), 'ctx', 'tensor'), parts along dimension 0
- w_qkv: bfloat16 [1024, 3, 1024], P(None, None, 'tensor')
- w_out: bfloat16 [1024, 1024], P('tensor'), may hold values from -0.1875 to 0.1875
- labels: int32 [4, 8, 1024], P(('groups', 'dp'), 'tensor', 'ctx'), parts along dimension 0, may hold values from 0 to 255, as said below
- grad_out: bfloat16 [4, 1024, 1024], P(('groups', 'dp'), 'ctx', 'tensor'), parts along dimension 0, may hold values from -6 to 6
Outputs:
- attended: bfloat16 [4, 1024, 1024], P(('groups', 'dp'), 'ctx', 'tensor'), parts along dimension 0
- grad_tokens: bfloat16 [4, 1024, 1024], P(('groups', 'dp'), 'ctx', 'tensor'), parts along dimension 0
- grad_w_qkv: float32 [2048, 3, 1024], P('groups', None, 'tensor'), parts along dimension 0
- grad_w_out: float32 [2048, 1024], P(('groups', 'tensor')), parts along dimension 0
There are 2 independent parts, one for each index of `groups`. A program takes and returns all parts, laid end to end along the dimension named above; an argument that names none is the same for every part. Nothing has to cross between parts.
Inputs may be any that keep to these rules, and one draw needn't show every extreme that they name: `labels`: cluster c of any head belongs to owner c % 4. Among the 256 tokens of one document on one index of ctx, at most 192 have, for one head, clusters of one owner; for each head one owner has exactly 192 from every such block, and the other owners share the rest of a block evenly (counts differ by at most one).
All inputs are finite; a program needn't handle non-finite values.
Results may differ from a plain program's by a relative error of at most 0.035.
The roundings to bfloat16 on the way count: a program that leaves them out, or rounds other values in their place, can miss the bound.
Values may be sent and summed in bfloat16 or wider, within the bound.
A program may use at most 64 MiB of HBM per device.

v0:
```python
import math
import jax
import jax.numpy as jnp
from jax import lax
from jax.sharding import PartitionSpec as P

HD = 128


def contract_last(left, right):
    return lax.dot_general(
        left, right, (((1,), (1,)), ((), ())), preferred_element_type=jnp.float32
    )


def contract_first(left, right):
    return lax.dot_general(
        left, right, (((0,), (0,)), ((), ())), preferred_element_type=jnp.float32
    )


def masked_probs(query_block, label_block, keys_in, marks):
    scores = contract_last(query_block, keys_in) * HD ** (-0.5)
    same = label_block[:, None] == marks[None, :]
    scores = jnp.where(same, scores, jnp.float32(-1e30))
    top_value = jnp.max(scores, axis=1, keepdims=True)
    expo = jnp.exp(scores - top_value)
    return expo / jnp.sum(expo, axis=1, keepdims=True)


def owner_forward(queries, keys_in, values_in, marks):
    total = queries.shape[0]
    block_rows = math.gcd(total, 512)
    block_count = total // block_rows

    def forward_block(index):
        start = index * block_rows
        query_block = lax.dynamic_slice_in_dim(queries, start, block_rows, 0)
        label_block = lax.dynamic_slice_in_dim(marks, start, block_rows, 0)
        probs = masked_probs(query_block, label_block, keys_in, marks).astype(jnp.bfloat16)
        return jnp.dot(probs, values_in, preferred_element_type=jnp.float32).astype(jnp.bfloat16)

    return lax.map(forward_block, jnp.arange(block_count, dtype=jnp.int32)).reshape(
        total, queries.shape[1]
    )


def owner_backward(queries, keys_in, values_in, marks, attention, cotangent):
    total, size = queries.shape
    block_rows = math.gcd(total, 512)
    block_count = total // block_rows

    def backward_block(carry, index):
        grad_keys, grad_values = carry
        start = index * block_rows
        query_block = lax.dynamic_slice_in_dim(queries, start, block_rows, 0)
        label_block = lax.dynamic_slice_in_dim(marks, start, block_rows, 0)
        attn_block = lax.dynamic_slice_in_dim(attention, start, block_rows, 0)
        cot_block = lax.dynamic_slice_in_dim(cotangent, start, block_rows, 0)
        probs_full = masked_probs(query_block, label_block, keys_in, marks)
        probs = probs_full.astype(jnp.bfloat16)
        dprob = contract_last(cot_block, values_in)
        delta = jnp.sum(
            cot_block.astype(jnp.float32) * attn_block.astype(jnp.float32), axis=1, keepdims=True
        )
        dscore = (probs_full * (dprob - delta) * HD ** (-0.5)).astype(jnp.bfloat16)
        grad_query = jnp.dot(dscore, keys_in, preferred_element_type=jnp.float32).astype(
            jnp.bfloat16
        )
        grad_keys = grad_keys + contract_first(dscore, query_block)
        grad_values = grad_values + contract_first(probs, cot_block)
        return ((grad_keys, grad_values), grad_query)

    empty = jnp.zeros((total, size), jnp.float32)
    (grad_keys, grad_values), grad_queries = lax.scan(
        backward_block, (empty, empty), jnp.arange(block_count, dtype=jnp.int32)
    )
    return (
        grad_queries.reshape(total, size),
        grad_keys.astype(jnp.bfloat16),
        grad_values.astype(jnp.bfloat16),
    )


def shards(tokens, w_qkv, w_out, labels, grad_out):
    rows_all, grads_all = (
        lax.all_gather(tokens, "tensor", axis=2, tiled=True),
        lax.all_gather(grad_out, "tensor", axis=2, tiled=True),
    )
    tok_rows = rows_all[0]
    tok_grads = grads_all[0]
    tok_count, width = tok_rows.shape
    heads_local = w_out.shape[0] // HD
    ctx_count = lax.axis_size("ctx")
    capacity = 3 * tok_count // ctx_count
    slot_total = ctx_count * capacity
    qkv = jnp.dot(
        tok_rows, w_qkv.reshape(width, 3 * heads_local * HD), preferred_element_type=jnp.float32
    )
    qkv = qkv.astype(jnp.bfloat16).reshape(tok_count, 3, heads_local, HD)
    qkv_heads = jnp.transpose(qkv, (2, 0, 1, 3)).reshape(heads_local, tok_count, 3 * HD)
    cotangent = contract_last(tok_grads, w_out).astype(jnp.bfloat16)
    cot_heads = jnp.transpose(cotangent.reshape(tok_count, heads_local, HD), (1, 0, 2))
    labels_local = labels[0]
    owner_of = labels_local % ctx_count
    owner_hits = (
        owner_of[:, :, None] == jnp.arange(ctx_count, dtype=jnp.int32)[None, None, :]
    ).astype(jnp.int32)
    earlier = jnp.cumsum(owner_hits, axis=1) - owner_hits
    slot_index = jnp.sum(earlier * owner_hits, axis=2)
    destination = owner_of * capacity + slot_index

    def pack(values):
        feature_count = values.shape[2]
        empty_buffer = jnp.zeros((heads_local, slot_total, feature_count), values.dtype)
        filled = jax.vmap(lambda buffer, where_to, rows_in: buffer.at[where_to].set(rows_in))(
            empty_buffer, destination, values
        )
        return filled.reshape(heads_local, ctx_count, capacity, feature_count)

    def unpack(received):
        flat = received.reshape(heads_local, slot_total, received.shape[3])
        return jax.vmap(lambda table, where_to: jnp.take(table, where_to, axis=0))(
            flat, destination
        )

    label_slots = jax.vmap(
        lambda where_to, marks: jnp.full((slot_total,), -1.0, jnp.bfloat16).at[where_to].set(marks)
    )(destination, labels_local.astype(jnp.bfloat16)).reshape(heads_local, ctx_count, capacity)
    arrived, arrived_marks = (
        lax.all_to_all(pack(qkv_heads), "ctx", split_axis=1, concat_axis=1, tiled=True),
        lax.all_to_all(label_slots, "ctx", split_axis=1, concat_axis=1, tiled=True),
    )
    arrived = arrived.reshape(heads_local, slot_total, 3 * HD)
    marks_own = arrived_marks.reshape(heads_local, slot_total)
    queries_own = arrived[:, :, :HD]
    keys_own = arrived[:, :, HD : 2 * HD]
    values_own = arrived[:, :, 2 * HD :]
    attention_own = jax.vmap(owner_forward)(queries_own, keys_own, values_own, marks_own)
    returned = lax.all_to_all(
        attention_own.reshape(heads_local, ctx_count, capacity, HD),
        "ctx",
        split_axis=1,
        concat_axis=1,
        tiled=True,
    )
    attention_tok = unpack(returned)
    cot_arrived = lax.all_to_all(pack(cot_heads), "ctx", split_axis=1, concat_axis=1, tiled=True)
    cot_own = cot_arrived.reshape(heads_local, slot_total, HD)
    grad_q, grad_k, grad_v = jax.vmap(owner_backward)(
        queries_own, keys_own, values_own, marks_own, attention_own, cot_own
    )
    grads_own = jnp.concatenate([grad_q, grad_k, grad_v], axis=2).reshape(
        heads_local, ctx_count, capacity, 3 * HD
    )
    grads_back = lax.all_to_all(grads_own, "ctx", split_axis=1, concat_axis=1, tiled=True)
    grad_heads = unpack(grads_back)
    attention_rows = jnp.transpose(attention_tok, (1, 0, 2)).reshape(tok_count, heads_local * HD)
    out_terms = jnp.dot(attention_rows, w_out, preferred_element_type=jnp.float32)
    attended = lax.psum_scatter(
        out_terms.astype(jnp.bfloat16), "tensor", scatter_dimension=1, tiled=True
    )
    grad_qkv = jnp.transpose(grad_heads.reshape(heads_local, tok_count, 3, HD), (1, 2, 0, 3))
    grad_qkv = grad_qkv.reshape(tok_count, 3 * heads_local * HD)
    grad_w_out_local = contract_first(attention_rows, tok_grads)
    grad_w_qkv_local = contract_first(tok_rows, grad_qkv).reshape(width, 3, heads_local * HD)
    summed_qkv, summed_out = (
        lax.psum(grad_w_qkv_local.astype(jnp.bfloat16), ("ctx", "dp")).astype(jnp.float32),
        lax.psum(grad_w_out_local.astype(jnp.bfloat16), ("ctx", "dp")).astype(jnp.float32),
    )
    in_terms = contract_last(grad_qkv, w_qkv.reshape(width, 3 * heads_local * HD))
    grad_tokens = lax.psum_scatter(
        in_terms.astype(jnp.bfloat16), "tensor", scatter_dimension=1, tiled=True
    )
    return (attended[None], grad_tokens[None], summed_qkv, summed_out)


def solution(mesh):
    placed = (
        P(("groups", "dp"), "ctx", "tensor"),
        P(None, None, "tensor"),
        P("tensor", None),
        P(("groups", "dp"), "tensor", "ctx"),
        P(("groups", "dp"), "ctx", "tensor"),
    )
    return jax.shard_map(
        shards,
        mesh=mesh,
        in_specs=placed,
        out_specs=(
            P(("groups", "dp"), "ctx", "tensor"),
            P(("groups", "dp"), "ctx", "tensor"),
            P("groups", None, "tensor"),
            P(("groups", "tensor"), None),
        ),
        check_vma=False,
    )
```

profile of v0, /device:TPU:0, one launch (start us, length us, event | category | flops | bytes accessed | tf_op | source)
XLA Modules:
  0.0 419.2 jit_solution(18375576288930993019)
XLA Ops:
  10.2 4.8 %reduce-window.6 = s32[4,4,2,128]{3,2,1,0:T(2,128)S(1)} reduce-window(s32[4,4,2,128]{3,2,1,0:T(2,128)S(1)} %compare_convert_fusion, s32[]{:T(128)} %constant.96.clone.1), window={size=1x1x1x128 pad=0_0x0_0x0_0x127_0}, to_apply=%region_0.1 | reduce-window | flops 520192 | bytes 32772 | tf_op jit(solution)/shard_map/reduce-window
  17.8 7.6 %scatter_custom_fusion = bf16[3072]{0:T(1024)(128)(2,1)S(1)} fusion(s32[1024]{0:T(1024)S(1)} %bitcast.228, bf16[1024]{0:T(1024)(128)(2,1)S(1)} %bitcast.231, bf16[]{:T(256)} %constant.103.clone.1), kind=kCustom, calls=%fused_computation.120 | custom fusion | bytes 6146
  26.1 6.3 %all-to-all-start = ((bf16[4,4,192]{2,0,1:T(4,128)(2,1)}), bf16[4,4,192]{2,0,1:T(4,128)(2,1)S(1)}, u32[]{:S(2)}, u32[]{:S(2)}) async-start(bf16[4,4,192]{2,0,1:T(4,128)(2,1)} %copy.67), calls=%async_computation | async-start | bytes 16384 | tf_op jit(solution)/shard_map/all_to_all | solution.py:132
  32.4 8.6 %all_gather.7 = bf16[1,256,1024]{2,1,0:T(8,128)(2,1)S(1)} all-gather(bf16[1,256,512]{2,1,0:T(8,128)(2,1)} %param.13), channel_id=1, replica_groups=mesh['groups'=2,'ctx'=4,'tensor'=2,'dp'=2] {'tensor'}, dimensions={2}, use_global_device_ids=true | all-gather | bytes 786432 | tf_op jit(solution)/shard_map/all_gather | solution.py:88
  42.4 3.4 scatter_custom_fusion.2
  45.8 0.9 copy.80
  46.8 4.8 %all-to-all-start.3 = ((bf16[4,4,192,128]{3,2,0,1:T(8,128)(2,1)}), bf16[4,4,192,128]{3,2,0,1:T(8,128)(2,1)}, u32[]{:S(2)}, u32[]{:S(2)}) async-start(bf16[4,4,192,128]{3,2,0,1:T(8,128)(2,1)} %copy.80), calls=%async_computation.4 | async-start | bytes 1572864 | tf_op jit(solution)/shard_map/all_to_all | solution.py:148
  51.6 4.7 %copy.69 = bf16[1024,3,512]{0,2,1:T(8,128)(2,1)} copy(bf16[1024,3,512]{2,0,1:T(8,128)(2,1)} %param.10) | data formatting | bytes 6291456 | tf_op args[1]
  56.3 7.0 %all_gather.6 = bf16[1,256,1024]{2,1,0:T(8,128)(2,1)S(1)} all-gather(bf16[1,256,512]{2,1,0:T(8,128)(2,1)S(1)} %copy-done.10), channel_id=1, replica_groups=mesh['groups'=2,'ctx'=4,'tensor'=2,'dp'=2] {'tensor'}, dimensions={2}, use_global_device_ids=true | all-gather | bytes 786432 | tf_op jit(solution)/shard_map/all_gather | solution.py:87
  64.1 2.9 convolution_convert_fusion.2
  68.2 1.2 copy.71
  69.3 6.5 %scatter_custom_fusion.1 = bf16[3072,384]{1,0:T(8,128)(2,1)S(1)} fusion(s32[1024]{0:T(1024)S(1)} %bitcast.230, bf16[1024,384]{1,0:T(8,128)(2,1)} %copy.71, bf16[]{:T(256)} %constant.102.clone.1), kind=kCustom, calls=%fused_computation.77 | custom fusion | bytes 2359808
  75.8 1.7 copy.72
  77.5 5.1 %all-to-all-start.1 = ((bf16[4,4,192,384]{3,2,0,1:T(8,128)(2,1)}), bf16[4,4,192,384]{3,2,0,1:T(8,128)(2,1)}, u32[]{:S(2)}, u32[]{:S(2)}) async-start(bf16[4,4,192,384]{3,2,0,1:T(8,128)(2,1)} %copy.72), calls=%async_computation.1 | async-start | bytes 4718592 | tf_op jit(solution)/shard_map/all_to_all | solution.py:131
  82.9 2.1 copy.81
  85.0 48.7 %all-to-all-done.1 = bf16[4,4,192,384]{3,2,0,1:T(8,128)(2,1)} async-done(((bf16[4,4,192,384]{3,2,0,1:T(8,128)(2,1)}), bf16[4,4,192,384]{3,2,0,1:T(8,128)(2,1)}, u32[]{:S(2)}, u32[]{:S(2)}) %all-to-all-start.1) | async-done | bytes 2359328 | tf_op jit(solution)/shard_map/all_to_all | solution.py:131
  133.7 1.9 copy.73
  135.6 1.6 fusion.105
  137.4 23.0 %while.33 = (s32[]{:T(128)}, bf16[3,4,256,128]{3,2,0,1:T(8,128)(2,1)S(1)}, s32[3]{0:T(128)S(1)}, bf16[4,768]{1,0:T(4,128)(2,1)S(1)}, bf16[4,4,192]{2,1,0:T(4,128...) while((s32[]{:T(128)}, ...), condition=%wide.wide.region_8.9_spmd, body=%wide.wide.region_5.8_spmd.sunk | while | flops 612764160 | bytes 3175139 | solution.py:43
  138.8 2.5 fusion.172
  141.3 3.8 fusion.173
  146.5 2.5 fusion.172
  149.0 3.8 fusion.173
  154.1 2.5 fusion.172
  156.6 3.8 fusion.173
  161.4 4.2 all-to-all-start.2
  165.6 1.1 broadcast.146.clone
  166.7 56.3 %while.34 = (s32[]{:T(128)}, f32[4,768,128]{2,1,0:T(8,128)S(1)}, f32[4,768,128]{2,1,0:T(8,128)}, bf16[3,4,256,128]{3,2,0,1:T(8,128)(2,1)}, s32[3]{0:T(128)S(1)},...) while((s32[]{:T(128)}, f32[4,768,128]{2,1,0:T(8,128)S(1)}, ...), condition=%wide.wide.region_15.16_spmd.clone, body=%wide.wide.region_11.15_spmd.clone.sunk | while | flops 1222772224 | bytes 25732404 | solution.py:75
  168.0 1.2 fusion.186
  169.2 4.1 fusion.187
  173.3 3.0 multiply_convert_fusion.3
  176.4 1.3 fusion.188
  177.6 2.2 select_add_fusion.6
  179.9 5.2 %select_add_fusion.7 = f32[4,768,128]{2,1,0:T(8,128)} fusion(f32[4,768,128]{2,1,0:T(8,128)} %get-tuple-element.590, f32[4,256]{1,0:T(4,128)S(1)} %get-tuple-element.527, pred[]{:T(512)S(6)} %compare.29, bf16[4,768,128]{2,1,0:T(8,128)(2,1)} %get-tuple-element.615, s32[]{:T(128)S(1)} %bitcast.226, ...), kind=kOutput, calls=%fused_computation.37.clone.clone.1 | convolution fusion | flops 408160000 | bytes 4469761 | tf_op jit(solution)/shard_map/vmap()/while/body/eval_jaxpr/dot_general | solution.py:17
  186.4 1.2 fusion.186
  187.6 4.1 fusion.187
  191.7 3.0 multiply_convert_fusion.3
  194.8 1.3 fusion.188
  196.0 2.2 select_add_fusion.6
  198.3 5.7 %select_add_fusion.7 = f32[4,768,128]{2,1,0:T(8,128)} fusion(f32[4,768,128]{2,1,0:T(8,128)} %get-tuple-element.590, f32[4,256]{1,0:T(4,128)S(1)} %get-tuple-element.527, pred[]{:T(512)S(6)} %compare.29, bf16[4,768,128]{2,1,0:T(8,128)(2,1)} %get-tuple-element.615, s32[]{:T(128)S(1)} %bitcast.226, ...), kind=kOutput, calls=%fused_computation.37.clone.clone.1 | convolution fusion | flops 408160000 | bytes 4469761 | tf_op jit(solution)/shard_map/vmap()/while/body/eval_jaxpr/dot_general | solution.py:17
  205.3 1.2 fusion.186
  206.6 4.1 fusion.187
  210.7 3.0 multiply_convert_fusion.3
  213.7 1.3 fusion.188
  215.0 2.2 select_add_fusion.6
  217.2 5.7 %select_add_fusion.7 = f32[4,768,128]{2,1,0:T(8,128)} fusion(f32[4,768,128]{2,1,0:T(8,128)} %get-tuple-element.590, f32[4,256]{1,0:T(4,128)S(1)} %get-tuple-element.527, pred[]{:T(512)S(6)} %compare.29, bf16[4,768,128]{2,1,0:T(8,128)(2,1)} %get-tuple-element.615, s32[]{:T(128)S(1)} %bitcast.226, ...), kind=kOutput, calls=%fused_computation.37.clone.clone.1 | convolution fusion | flops 408160000 | bytes 4469761 | tf_op jit(solution)/shard_map/vmap()/while/body/eval_jaxpr/dot_general | solution.py:17
  223.1 1.3 copy-done.8
  224.5 1.5 pad_maximum_fusion
  226.0 1.7 copy.84
  227.6 5.2 %all-to-all-start.4 = ((bf16[4,4,192,384]{3,2,0,1:T(8,128)(2,1)}), bf16[4,4,192,384]{3,2,0,1:T(8,128)(2,1)}, u32[]{:S(2)}, u32[]{:S(2)}) async-start(bf16[4,4,192,384]{3,2,0,1:T(8,128)(2,1)} %copy.84), calls=%async_computation.5 | async-start | bytes 4718592 | tf_op jit(solution)/shard_map/all_to_all | solution.py:156
  232.9 1.2 copy.77
  234.1 5.8 %gather_fusion = bf16[1024,128]{1,0:T(8,128)(2,1)S(1)} fusion(bf16[4,768,128]{2,1,0:T(8,128)(2,1)S(1)} %bitcast.205, s32[1024]{0:T(1024)S(1)} %bitcast.199), kind=kCustom, calls=%fused_computation | custom fusion | bytes 532480 | tf_op jit(solution)/shard_map/vmap(jit(_take))/gather | solution.py:123
  240.9 1.4 convolution_convert_fusion.3
  242.3 43.4 %all-to-all-done.4 = bf16[4,4,192,384]{3,2,0,1:T(8,128)(2,1)} async-done(((bf16[4,4,192,384]{3,2,0,1:T(8,128)(2,1)}), bf16[4,4,192,384]{3,2,0,1:T(8,128)(2,1)}, u32[]{:S(2)}, u32[]{:S(2)}) %all-to-all-start.4) | async-done | bytes 2359328 | tf_op jit(solution)/shard_map/all_to_all | solution.py:156
  285.7 1.9 copy.85
  287.6 11.6 %gather_fusion.1 = bf16[1024,384]{1,0:T(8,128)(2,1)} fusion(bf16[4,768,384]{2,1,0:T(8,128)(2,1)S(1)} %bitcast.201, s32[1024]{0:T(1024)S(1)} %bitcast.200), kind=kCustom, calls=%fused_computation.1 | custom fusion | bytes 1581056 | tf_op jit(solution)/shard_map/vmap(jit(_take))/gather | solution.py:123
  299.2 1.5 copy.86
  301.7 2.7 convolution_convert_fusion.1
  304.4 4.7 %copy.88 = bf16[1024,3,512]{2,0,1:T(8,128)(2,1)} copy(bf16[1024,3,512]{0,2,1:T(8,128)(2,1)} %bitcast.202) | data formatting | bytes 6291456 | tf_op jit(solution)/shard_map/convert_element_type | solution.py:168
  310.0 1.3 convolution_convert_fusion.4
  311.3 3.7 convolution_convert_fusion.5
  315.1 90.2 %all-reduce.3.cloned.1.call-done = (bf16[1024,3,512]{2,0,1:T(8,128)(2,1)}, bf16[512,1024]{1,0:T(8,128)(2,1)}) async-done(((bf16[1024,3,512]{2,0,1:T(8,128)(2,1)}, bf16[512,1024]{1,0:T(8,128)(2,1)}), (bf16[1024,3,512]{2,0,1:T(8,128)(2,1)}, bf16[512,1024]{1,0:T(8,128)(2,1)})) %all-reduce.3.cloned.1.call-update) | async-done | bytes 4194320 | tf_op jit(solution)/shard_map/psum | solution.py:168
  405.3 2.9 convert_element_type.81
  408.2 3.6 convert_element_type.79
  (104 shorter events, 17.5 us)
Async XLA Ops:
  8.0 33.8 %copy-start = (bf16[512,1024]{1,0:T(8,128)(2,1)S(1)}, bf16[512,1024]{1,0:T(8,128)(2,1)}, u32[]{:S(2)}) copy-start(bf16[512,1024]{1,0:T(8,128)(2,1)} %param.11) | copy-start | bytes 3145732
  26.1 20.7 %all-to-all-start = ((bf16[4,4,192]{2,0,1:T(4,128)(2,1)}), bf16[4,4,192]{2,0,1:T(4,128)(2,1)S(1)}, u32[]{:S(2)}, u32[]{:S(2)}) async-start(bf16[4,4,192]{2,0,1:T(4,128)(2,1)} %copy.67), calls=%async_computation | async-start | bytes 16384 | tf_op jit(solution)/shard_map/all_to_all | solution.py:132
  41.0 0.8 copy-start.1
  46.8 30.7 %all-to-all-start.3 = ((bf16[4,4,192,128]{3,2,0,1:T(8,128)(2,1)}), bf16[4,4,192,128]{3,2,0,1:T(8,128)(2,1)}, u32[]{:S(2)}, u32[]{:S(2)}) async-start(bf16[4,4,192,128]{3,2,0,1:T(8,128)(2,1)} %copy.80), calls=%async_computation.4 | async-start | bytes 1572864 | tf_op jit(solution)/shard_map/all_to_all | solution.py:148
  51.6 4.7 %copy-start.10 = (bf16[1,256,512]{2,1,0:T(8,128)(2,1)S(1)}, bf16[1,256,512]{2,1,0:T(8,128)(2,1)}, u32[]{:S(2)}) copy-start(bf16[1,256,512]{2,1,0:T(8,128)(2,1)} %param.9) | copy-start | bytes 786436
  63.3 0.8 copy-start.6
  77.5 56.2 %all-to-all-start.1 = ((bf16[4,4,192,384]{3,2,0,1:T(8,128)(2,1)}), bf16[4,4,192,384]{3,2,0,1:T(8,128)(2,1)}, u32[]{:S(2)}, u32[]{:S(2)}) async-start(bf16[4,4,192,384]{3,2,0,1:T(8,128)(2,1)} %copy.72), calls=%async_computation.1 | async-start | bytes 4718592 | tf_op jit(solution)/shard_map/all_to_all | solution.py:131
  82.6 53.0 %copy-start.11 = (bf16[4,4,192]{2,1,0:T(4,128)(2,1)}, bf16[4,4,192]{2,1,0:T(4,128)(2,1)S(1)}, u32[]{:S(2)}) copy-start(bf16[4,4,192]{2,1,0:T(4,128)(2,1)S(1)} %copy.68) | copy-start | bytes 18436
  161.4 66.2 %all-to-all-start.2 = ((bf16[4,4,192,128]{3,2,0,1:T(8,128)(2,1)}), bf16[4,4,192,128]{3,2,0,1:T(8,128)(2,1)}, u32[]{:S(2)}, u32[]{:S(2)}) async-start(bf16[4,4,192,128]{3,2,0,1:T(8,128)(2,1)} %copy.76), calls=%async_computation.2 | async-start | bytes 1572864 | tf_op jit(solution)/shard_map/all_to_all | solution.py:140
  173.3 3.0 copy-start.9
  191.7 3.0 copy-start.9
  210.7 3.0 copy-start.9
  223.0 1.4 copy-start.8
  227.6 5.2 %copy-start.12 = (s32[1,4,256]{2,1,0:T(4,128)S(1)}, s32[1,4,256]{2,1,0:T(4,128)}, u32[]{:S(2)}) copy-start(s32[1,4,256]{2,1,0:T(4,128)} %param.12) | copy-start | bytes 12292
  227.6 58.0 %all-to-all-start.4 = ((bf16[4,4,192,384]{3,2,0,1:T(8,128)(2,1)}), bf16[4,4,192,384]{3,2,0,1:T(8,128)(2,1)}, u32[]{:S(2)}, u32[]{:S(2)}) async-start(bf16[4,4,192,384]{3,2,0,1:T(8,128)(2,1)} %copy.84), calls=%async_computation.5 | async-start | bytes 4718592 | tf_op jit(solution)/shard_map/all_to_all | solution.py:156
  232.8 8.0 %copy-start.2 = (bf16[1,256,1024]{2,1,0:T(8,128)(2,1)S(1)}, bf16[1,256,1024]{2,1,0:T(8,128)(2,1)}, u32[]{:S(2)}) copy-start(bf16[1,256,1024]{2,1,0:T(8,128)(2,1)} %copy-done.1) | copy-start | bytes 1572868
  232.8 172.4 %all-reduce.3.cloned.1.call-start = ((), (), s32[]{:S(2)}) async-start(), calls=%async_computation.9 | async-start | bytes 8388608 | tf_op jit(solution)/shard_map/psum | solution.py:168
  240.2 0.7 copy-start.4
  299.2 2.5 copy-start.7
  309.1 0.9 copy-start.5
  309.1 102.7 %reduce-scatter.3.cloned.1.call-start = ((), (), s32[]{:S(2)}) async-start(), calls=%async_computation.7 | async-start | bytes 786432 | tf_op jit(solution)/shard_map/reduce_scatter | solution.py:160
  311.3 100.5 %reduce-scatter.5.cloned.1.call-start = ((), (), s32[]{:S(2)}) async-start(), calls=%async_computation.8 | async-start | bytes 786432 | tf_op jit(solution)/shard_map/reduce_scatter | solution.py:172
  405.2 2.9 copy-start.3
Sparse Core Ops, SparseCore 0:
  309.2 95.9 all-reduce.2
Sparse Core Ops, SparseCore 1:
  312.4 13.6 reduce-scatter.2
  328.8 14.5 reduce-scatter.4
where the time goes:
time: 421 us; the launch traced here: 419 us
  waiting for transfers between devices  182 us (43%)
  matrix products  80 us (19%)
  local copies, waits for them, and re-layouts  74.3 us (18%)
  starting transfers between devices  25.7 us (6%)
  other arithmetic  21.4 us (5%)
  between operations  15.8 us (4%)
  blocking collectives  15.7 us (4%)
    psum x1, waiting for transfers between devices, shards(): lax.psum(grad_w_qkv_local.astype(jnp.bfloat16), ('ctx', 'dp'))  90.2 us
    all_to_all x1, waiting for transfers between devices, shards(): lax.all_to_all(pack(qkv_heads), 'ctx', split_axis=1, concat_axis=1, tiled...  48.7 us
    all_to_all x1, waiting for transfers between devices, shards(): lax.all_to_all(grads_own, 'ctx', split_axis=1, concat_axis=1, tiled=True)  43.4 us
    dot_general x8, matrix products, contract_first(): lax.dot_general(left, right, (((0,), (0,)), ((), ())), preferred_element_...  27.5 us
    unnamed x32, local copies, waits for them, and re-layouts  26.9 us
    sub x6, matrix products, masked_probs(): expo = jnp.exp(scores - top_value)  19.8 us
    gather x5, local copies, waits for them, and re-layouts, unpack(): jnp.take(table, where_to, axis=0)  19.6 us
    dot_general x5, matrix products, contract_last(): lax.dot_general(left, right, (((1,), (1,)), ((), ())), preferred_element_...  13.2 us
  transfers between devices with their start and end apart: 8, of which 3 were waited for; matrix products, arithmetic and copies ran while one was open for 25% of the time, Pallas kernels for 0%

commit v1 on v0

--- a/solution.py
+++ b/solution.py
@@ -165,7 +165,9 @@
     grad_w_out_local = contract_first(attention_rows, tok_grads)
     grad_w_qkv_local = contract_first(tok_rows, grad_qkv).reshape(width, 3, heads_local * HD)
     summed_qkv, summed_out = (
-        lax.psum(grad_w_qkv_local.astype(jnp.bfloat16), ("ctx", "dp")).astype(jnp.float32),
+        jnp.sum(
+            lax.all_gather(grad_w_qkv_local.astype(jnp.bfloat16), ("ctx", "dp")), axis=0
+        ).astype(jnp.float32),
         lax.psum(grad_w_out_local.astype(jnp.bfloat16), ("ctx", "dp")).astype(jnp.float32),
     )
     in_terms = contract_last(grad_qkv, w_qkv.reshape(width, 3 * heads_local * HD))

time: 421 us -> 589 us (1.40)
  waiting for transfers between devices: 182 us -> 321 us
  other arithmetic: 21.4 us -> 33.2 us
  matrix products: 80 us -> 89.4 us
  local copies, waits for them, and re-layouts: 74.3 us -> 82.4 us
    all_gather x0 -> x1, waiting for transfers between devices: none -> 218 us  [shards(): lax.all_gather(grad_w_qkv_local.astype(jnp.bfloat16), ('ctx', 'dp'))]
    psum x1, waiting for transfers between devices: 90.2 us -> 0.68 us  [shards(): lax.psum(grad_w_out_local.astype(jnp.bfloat16), ('ctx', 'dp'))]
    reduce_sum x0 -> x1, other arithmetic: none -> 15.3 us  [shards(): jnp.sum(lax.all_gather(grad_w_qkv_local.astype(jnp.bfloat16), ('ctx', 'dp...]
    all_to_all x1, waiting for transfers between devices: 43.4 us -> 53.6 us  [shards(): lax.all_to_all(grads_own, 'ctx', split_axis=1, concat_axis=1, tiled=True)]
    unnamed x32, local copies, waits for them, and re-layouts: 26.9 us -> 34.9 us
  transfers between devices with their start and end apart: 8 -> 9, of which waited for: 3 -> 4; matrix products, arithmetic and copies ran while one was open for 25% -> 27% of each run, Pallas kernels for 0% -> 0%
where the time goes in v1:
time: 589 us; the launch traced here: 587 us
  waiting for transfers between devices  321 us (54%)
  matrix products  89.4 us (15%)
  local copies, waits for them, and re-layouts  82.4 us (14%)
  other arithmetic  33.2 us (6%)
  starting transfers between devices  25.9 us (4%)
  between operations  15.8 us (3%)
  blocking collectives  15.7 us (3%)
    all_gather x1, waiting for transfers between devices, shards(): lax.all_gather(grad_w_qkv_local.astype(jnp.bfloat16), ('ctx', 'dp'))  218 us
    all_to_all x1, waiting for transfers between devices, shards(): lax.all_to_all(grads_own, 'ctx', split_axis=1, concat_axis=1, tiled=True)  53.6 us
    all_to_all x1, waiting for transfers between devices, shards(): lax.all_to_all(pack(qkv_heads), 'ctx', split_axis=1, concat_axis=1, tiled...  48.8 us
    unnamed x32, local copies, waits for them, and re-layouts  34.9 us
    dot_general x8, matrix products, contract_first(): lax.dot_general(left, right, (((0,), (0,)), ((), ())), preferred_element_...  28.7 us
    sub x6, matrix products, masked_probs(): expo = jnp.exp(scores - top_value)  19.9 us
    gather x5, local copies, waits for them, and re-layouts, unpack(): jnp.take(table, where_to, axis=0)  19.6 us
    dot_general x5, matrix products, contract_last(): lax.dot_general(left, right, (((1,), (1,)), ((), ())), preferred_element_...  16.6 us
  transfers between devices with their start and end apart: 9, of which 4 were waited for; matrix products, arithmetic and copies ran while one was open for 27% of the time, Pallas kernels for 0%

profile of v1, /device:TPU:0, one launch (start us, length us, event | category | flops | bytes accessed | tf_op | source)
XLA Modules:
  0.0 587.3 jit_solution(12248956988960880550)
XLA Ops:
  10.2 4.8 reduce-window.6
  17.8 7.6 %scatter_custom_fusion = bf16[3072]{0:T(1024)(128)(2,1)S(1)} fusion(s32[1024]{0:T(1024)S(1)} %bitcast.226, bf16[1024]{0:T(1024)(128)(2,1)S(1)} %bitcast.229, bf16[]{:T(256)} %constant.105.clone.1), kind=kCustom, calls=%fused_computation.120 | custom fusion | bytes 6146
  26.1 6.3 %all-to-all-start = ((bf16[4,4,192]{2,0,1:T(4,128)(2,1)}), bf16[4,4,192]{2,0,1:T(4,128)(2,1)S(1)}, u32[]{:S(2)}, u32[]{:S(2)}) async-start(bf16[4,4,192]{2,0,1:T(4,128)(2,1)} %copy.66), calls=%async_computation | async-start | bytes 16384 | tf_op jit(solution)/shard_map/all_to_all | solution.py:132
  32.4 8.6 %all_gather.11 = bf16[1,256,1024]{2,1,0:T(8,128)(2,1)S(1)} all-gather(bf16[1,256,512]{2,1,0:T(8,128)(2,1)} %param.13), channel_id=1, replica_groups=mesh['groups'=2,'ctx'=4,'tensor'=2,'dp'=2] {'tensor'}, dimensions={2}, use_global_device_ids=true | all-gather | bytes 786432 | tf_op jit(solution)/shard_map/all_gather | solution.py:88
  42.4 3.4 scatter_custom_fusion.2
  46.8 4.8 all-to-all-start.3
  51.6 4.7 copy.68
  56.3 7.0 %all_gather.10 = bf16[1,256,1024]{2,1,0:T(8,128)(2,1)S(1)} all-gather(bf16[1,256,512]{2,1,0:T(8,128)(2,1)S(1)} %copy-done.8), channel_id=1, replica_groups=mesh['groups'=2,'ctx'=4,'tensor'=2,'dp'=2] {'tensor'}, dimensions={2}, use_global_device_ids=true | all-gather | bytes 786432 | tf_op jit(solution)/shard_map/all_gather | solution.py:87
  64.1 2.9 convolution_convert_fusion.2
  68.1 1.2 copy.70
  69.3 6.5 %scatter_custom_fusion.1 = bf16[3072,384]{1,0:T(8,128)(2,1)S(1)} fusion(s32[1024]{0:T(1024)S(1)} %bitcast.228, bf16[1024,384]{1,0:T(8,128)(2,1)} %copy.70, bf16[]{:T(256)} %constant.104.clone.1), kind=kCustom, calls=%fused_computation.77 | custom fusion | bytes 2359808
  75.8 1.7 copy.71
  77.5 5.1 all-to-all-start.1
  82.8 2.1 copy.80
  84.9 48.8 %all-to-all-done.1 = bf16[4,4,192,384]{3,2,0,1:T(8,128)(2,1)} async-done(((bf16[4,4,192,384]{3,2,0,1:T(8,128)(2,1)}), bf16[4,4,192,384]{3,2,0,1:T(8,128)(2,1)}, u32[]{:S(2)}, u32[]{:S(2)}) %all-to-all-start.1) | async-done | bytes 2359328 | tf_op jit(solution)/shard_map/all_to_all | solution.py:131
  133.7 1.9 copy.72
  135.6 1.6 fusion.105
  137.3 23.1 %while.33 = (s32[]{:T(128)}, bf16[3,4,256,128]{3,2,0,1:T(8,128)(2,1)S(1)}, s32[3]{0:T(128)S(1)}, bf16[4,768]{1,0:T(4,128)(2,1)S(1)}, bf16[4,4,192]{2,1,0:T(4,128...) while((s32[]{:T(128)}, ...), condition=%wide.wide.region_8.9_spmd, body=%wide.wide.region_5.8_spmd.sunk | while | flops 612764160 | bytes 3175139 | solution.py:43
  138.7 2.5 fusion.172
  141.2 3.8 fusion.173
  146.4 2.5 fusion.172
  148.9 3.8 fusion.173
  154.1 2.5 fusion.172
  156.6 3.8 fusion.173
  160.4 1.0 copy.75
  161.4 4.2 all-to-all-start.2
  166.7 65.6 %while.34 = (s32[]{:T(128)}, f32[4,768,128]{2,1,0:T(8,128)S(1)}, f32[4,768,128]{2,1,0:T(8,128)}, bf16[3,4,256,128]{3,2,0,1:T(8,128)(2,1)}, s32[3]{0:T(128)S(1)},...) while((s32[]{:T(128)}, f32[4,768,128]{2,1,0:T(8,128)S(1)}, ...), condition=%wide.wide.region_15.16_spmd.clone, body=%wide.wide.region_11.15_spmd.clone.sunk | while | flops 1222772224 | bytes 22586648 | solution.py:75
  168.0 1.2 fusion.186
  169.2 4.1 fusion.187
  173.3 4.1 multiply_convert_fusion.3
  177.5 2.7 select_add_fusion.6
  180.1 5.2 select_add_fusion.7
  185.3 2.9 fusion.188
  189.5 1.2 fusion.186
  190.7 4.1 fusion.187
  194.8 4.1 multiply_convert_fusion.3
  199.0 2.7 select_add_fusion.6
  201.6 5.7 select_add_fusion.7
  207.4 2.9 fusion.188
  211.6 1.2 fusion.186
  212.8 4.1 fusion.187
  216.9 4.1 multiply_convert_fusion.3
  221.0 2.7 select_add_fusion.6
  223.7 5.7 select_add_fusion.7
  229.4 2.9 fusion.188
  232.3 1.6 convert_element_type.83
  234.4 1.7 copy.83
  236.0 5.2 all-to-all-start.4
  241.2 1.2 copy.76
  242.5 5.8 gather_fusion
  248.5 1.4 convolution_convert_fusion.3
  250.3 53.6 %all-to-all-done.4 = bf16[4,4,192,384]{3,2,0,1:T(8,128)(2,1)} async-done(((bf16[4,4,192,384]{3,2,0,1:T(8,128)(2,1)}), bf16[4,4,192,384]{3,2,0,1:T(8,128)(2,1)}, u32[]{:S(2)}, u32[]{:S(2)}) %all-to-all-start.4) | async-done | bytes 2359328 | tf_op jit(solution)/shard_map/all_to_all | solution.py:156
  303.9 1.9 copy.84
  305.8 11.6 %gather_fusion.1 = bf16[1024,384]{1,0:T(8,128)(2,1)} fusion(bf16[4,768,384]{2,1,0:T(8,128)(2,1)S(1)} %bitcast.198, s32[1024]{0:T(1024)S(1)} %bitcast.197), kind=kCustom, calls=%fused_computation.1 | custom fusion | bytes 1581056 | tf_op jit(solution)/shard_map/vmap(jit(_take))/gather | solution.py:123
  317.4 1.5 copy.85
  319.9 2.7 convolution_convert_fusion.1
  322.6 4.7 copy.87
  328.2 1.3 convolution_convert_fusion.4
  329.6 3.8 convolution_convert_fusion.5
  334.1 2.8 convert_element_type.90
  336.8 217.7 %all-gather.2.cloned.1.call-done = bf16[8,1024,3,512]{3,1,2,0:T(8,128)(2,1)} async-done(((bf16[1,1024,3,512]{3,1,2,0:T(8,128)(2,1)}), bf16[8,1024,3,512]{3,1,2,0:T(8,128)(2,1)}) %all-gather.2.cloned.1.call-update) | async-done | bytes 25165840 | tf_op jit(solution)/shard_map/all_gather | solution.py:169
  554.6 15.3 %reduce_sum.52 = bf16[1024,3,512]{2,0,1:T(8,128)(2,1)} reduce(bf16[8,1024,3,512]{3,1,2,0:T(8,128)(2,1)} %all-gather.2.cloned.1.call-done, bf16[]{:T(256)} %constant.104.clone.1), dimensions={0}, to_apply=%region_17.18 | reduce | flops 11010048 | bytes 28311554 | tf_op jit(solution)/shard_map/reduce_sum | solution.py:168
  569.8 4.7 copy.96
  574.5 5.4 copy.89
  (101 shorter events, 19.0 us)
Async XLA Ops:
  8.0 33.8 %copy-start = (bf16[512,1024]{1,0:T(8,128)(2,1)S(1)}, bf16[512,1024]{1,0:T(8,128)(2,1)}, u32[]{:S(2)}) copy-start(bf16[512,1024]{1,0:T(8,128)(2,1)} %param.11) | copy-start | bytes 3145732
  26.1 20.7 %all-to-all-start = ((bf16[4,4,192]{2,0,1:T(4,128)(2,1)}), bf16[4,4,192]{2,0,1:T(4,128)(2,1)S(1)}, u32[]{:S(2)}, u32[]{:S(2)}) async-start(bf16[4,4,192]{2,0,1:T(4,128)(2,1)} %copy.66), calls=%async_computation | async-start | bytes 16384 | tf_op jit(solution)/shard_map/all_to_all | solution.py:132
  41.0 0.8 copy-start.1
  46.8 30.7 %all-to-all-start.3 = ((bf16[4,4,192,128]{3,2,0,1:T(8,128)(2,1)}), bf16[4,4,192,128]{3,2,0,1:T(8,128)(2,1)}, u32[]{:S(2)}, u32[]{:S(2)}) async-start(bf16[4,4,192,128]{3,2,0,1:T(8,128)(2,1)} %copy.79), calls=%async_computation.4 | async-start | bytes 1572864 | tf_op jit(solution)/shard_map/all_to_all | solution.py:148
  51.6 4.7 copy-start.8
  63.3 0.8 copy-start.6
  77.5 56.2 %all-to-all-start.1 = ((bf16[4,4,192,384]{3,2,0,1:T(8,128)(2,1)}), bf16[4,4,192,384]{3,2,0,1:T(8,128)(2,1)}, u32[]{:S(2)}, u32[]{:S(2)}) async-start(bf16[4,4,192,384]{3,2,0,1:T(8,128)(2,1)} %copy.71), calls=%async_computation.1 | async-start | bytes 4718592 | tf_op jit(solution)/shard_map/all_to_all | solution.py:131
  82.6 53.0 %copy-start.9 = (bf16[4,4,192]{2,1,0:T(4,128)(2,1)}, bf16[4,4,192]{2,1,0:T(4,128)(2,1)S(1)}, u32[]{:S(2)}) copy-start(bf16[4,4,192]{2,1,0:T(4,128)(2,1)S(1)} %copy.67) | copy-start | bytes 18436
  161.4 74.6 %all-to-all-start.2 = ((bf16[4,4,192,128]{3,2,0,1:T(8,128)(2,1)}), bf16[4,4,192,128]{3,2,0,1:T(8,128)(2,1)}, u32[]{:S(2)}, u32[]{:S(2)}) async-start(bf16[4,4,192,128]{3,2,0,1:T(8,128)(2,1)} %copy.75), calls=%async_computation.2 | async-start | bytes 1572864 | tf_op jit(solution)/shard_map/all_to_all | solution.py:140
  232.3 1.7 copy-start.3
  236.0 5.2 copy-start.10
  236.0 67.9 %all-to-all-start.4 = ((bf16[4,4,192,384]{3,2,0,1:T(8,128)(2,1)}), bf16[4,4,192,384]{3,2,0,1:T(8,128)(2,1)}, u32[]{:S(2)}, u32[]{:S(2)}) async-start(bf16[4,4,192,384]{3,2,0,1:T(8,128)(2,1)} %copy.83), calls=%async_computation.5 | async-start | bytes 4718592 | tf_op jit(solution)/shard_map/all_to_all | solution.py:156
  241.2 7.3 %copy-start.2 = (bf16[1,256,1024]{2,1,0:T(8,128)(2,1)S(1)}, bf16[1,256,1024]{2,1,0:T(8,128)(2,1)}, u32[]{:S(2)}) copy-start(bf16[1,256,1024]{2,1,0:T(8,128)(2,1)} %copy-done.1) | copy-start | bytes 1572868
  241.2 92.9 %all-reduce.2.cloned.1.call-start = ((), (), s32[]{:S(2)}) async-start(), calls=%async_computation.10 | async-start | bytes 2097152 | tf_op jit(solution)/shard_map/psum | solution.py:171
  248.5 1.7 copy-start.4
  250.0 304.6 %all-gather.2.cloned.1.call-start = ((), (), s32[]{:S(2)}) async-start(), calls=%async_computation.9 | async-start | bytes 28311552 | tf_op jit(solution)/shard_map/all_gather | solution.py:169
  317.4 2.5 copy-start.7
  327.3 0.9 copy-start.5
  327.3 252.6 %reduce-scatter.3.cloned.1.call-start = ((), (), s32[]{:S(2)}) async-start(), calls=%async_computation.7 | async-start | bytes 786432 | tf_op jit(solution)/shard_map/reduce_scatter | solution.py:160
  329.5 250.4 %reduce-scatter.5.cloned.1.call-start = ((), (), s32[]{:S(2)}) async-start(), calls=%async_computation.8 | async-start | bytes 786432 | tf_op jit(solution)/shard_map/reduce_scatter | solution.py:174
Sparse Core Ops, SparseCore 0:
  250.1 83.9 all-reduce.1
  335.7 218.8 all-gather.1
Sparse Core Ops, SparseCore 1:
  330.6 13.5 reduce-scatter.2
  346.9 14.5 reduce-scatter.4
